TPU v7x, 256 devices: a whole 4x4x8 slice. The times are simulated.
256 devices in a mesh: seq: 32 (over x, y, core), mp: 8 (over z).
Axes of the slice: x: 4, y: 4, z: 8, core: 2. Of those that a mesh axis runs over, the one named last changes fastest.
Arguments:
- x_branch: bfloat16 [8192, 8192], P('seq', 'mp'), may hold values from -6 to 6
- z_branch: bfloat16 [8192, 8192], P('seq', 'mp'), may hold values from -6 to 6
- conv_weight: float32 [4, 8192], P(None, 'mp'), may hold values from -3 to 3
- conv_bias: float32 [8192], P('mp'), may hold values from -0.5 to 0.5
- xproj_weight: bfloat16 [8192, 544], P('mp'), may hold values from -0.0625 to 0.0625
- dt_weight: bfloat16 [512, 8192], P(None, 'mp'), may hold values from -0.25 to 0.25
- dt_bias: float32 [8192], P('mp'), may hold values from -4 to -2
- decay_rate: float32 [16, 8192], P(None, 'mp'), may hold values from 0.00024414062 to 2
- skip_gain: float32 [8192], P('mp'), may hold values from 0.5 to 1.5
- query_rows: bfloat16 [8192, 8192], P('seq', 'mp'), may hold values from -6 to 6
- key_rows: bfloat16 [8192, 1024], P('seq', 'mp'), may hold values from -6 to 6
- value_rows: bfloat16 [8192, 1024], P('seq', 'mp'), may hold values from -6 to 6
- lengths: int32 [4], replicated, may hold values from 1 to 4096, as said below
- destination: int32 [8192], replicated, may hold values from 0 to 8191, as said below
Outputs:
- mamba_out: bfloat16 [8192, 8192], P('seq', 'mp')
- regrouped: bfloat16 [8192, 8192], P('seq', 'mp')
Inputs may be any that keep to these rules, and one draw needn't show every extreme that they name: The 4 lengths sum to 8192, and the second of them equals 4096. destination is a permutation of 0 to 8191. Cut each aligned block of 256 positions into 32 runs of 8 consecutive positions: each run goes in order to consecutive rows of one aligned target block, the runs of block i to the rows that start at i * 8 within their target blocks, and the 32 runs of one block go to 32 different target blocks.
All inputs are finite; a program needn't handle non-finite values.
Results may differ from a plain program's by a relative error of at most 0.02.
Values may be sent and summed in bfloat16 or wider, within the bound.
A program may use at most 128 MiB of HBM per device.

v0:
```python
import math

import jax
import jax.numpy as jnp
from jax import lax
from jax.experimental import pallas as pl
from jax.experimental.pallas import tpu as pltpu
from jax.sharding import Mesh
from jax.sharding import PartitionSpec as P

SEQ = ("seq_0", "seq_1", "seq_2")
MESH = pl.DeviceIdType.MESH
VM = pltpu.VMEM
F32 = jnp.float32
BF16 = jnp.bfloat16
LOG2E = math.log2(math.e)
NX, NY, NC, NZ = 4, 4, 2, 8
NSEQ = NX * NY * NC
TOK = 256
TOK_BITS = 8
TOKENS = NSEQ * TOK
CH = 1024
LANE = 128
SUB = CH // LANE
NS = 16
RANK = 512
PROJ = RANK + 2 * NS
HD = 128
TAPS = 4
BIG_STEP = 1.0e7
MASKED = -1.0e30
GROUP = 8
RUN = TOK // NSEQ
BK = 512
VLIM = 60 * 1024 * 1024


def whole(space=VM):
    return pl.BlockSpec(memory_space=space)


def place():
    return (
        lax.axis_index("seq_0"),
        lax.axis_index("seq_1"),
        lax.axis_index("seq_2"),
        lax.axis_index("mp"),
    )


def seq_device(j, z):
    chip = lax.div(j, NC)
    return (lax.div(chip, NY), lax.rem(chip, NY), lax.rem(j, NC), z)


def doc_starts(len_ref):
    s1 = len_ref[0]
    s2 = s1 + len_ref[1]
    return s1, s2, s2 + len_ref[2]


def start_of(pos, starts):
    s1, s2, s3 = starts
    return jnp.where(pos >= s3, s3, jnp.where(pos >= s2, s2, jnp.where(pos >= s1, s1, 0)))


def silu(x):
    half = 0.5 * x
    return half * jnp.tanh(half) + half


def mixer_kernel(
    dest_ref,
    len_ref,
    q_ref,
    k_ref,
    v_ref,
    x_ref,
    z_hbm,
    cw_ref,
    cb_ref,
    xw_hbm,
    dtw_hbm,
    dtb_ref,
    rate_ref,
    skip_ref,
    q_out,
    kv_out,
    pos_out,
    out,
    kvs,
    qs,
    halo,
    ext,
    inner,
    part,
    rs_plus,
    rs_minus,
    go_plus,
    go_minus,
    proj,
    steps,
    drives,
    rates,
    spread,
    gains,
    ys,
    sums,
    st_own,
    st_pair,
    st_y,
    st_x,
    decays,
    z_ref,
    xw_ref,
    dtw_ref,
    loc_sem,
    halo_sem,
    kv_send,
    kv_recv,
    q_send,
    q_recv,
    rs_send,
    rs_recv,
    ag_send,
    ag_recv,
    st_send,
    st_recv,
):
    x, y, c, z = place()
    me = (x * NY + y) * NC + c
    anchor = me * TOK
    barrier = pltpu.get_barrier_semaphore()
    for k in range(1, NSEQ):
        pl.semaphore_signal(
            barrier, inc=1, device_id=seq_device(lax.rem(me + k, NSEQ), z), device_id_type=MESH
        )
    for k in range(1, NZ):
        pl.semaphore_signal(
            barrier, inc=1, device_id=(x, y, c, lax.rem(z + k, NZ)), device_id_type=MESH
        )
    load_k = pltpu.make_async_copy(k_ref, kvs.at[:, pl.ds(0, HD)], loc_sem.at[0])
    load_k.start()
    load_x = pltpu.make_async_copy(xw_hbm, xw_ref, loc_sem.at[2])
    load_x.start()
    load_d = pltpu.make_async_copy(dtw_hbm, dtw_ref, loc_sem.at[3])
    load_d.start()
    load_z = pltpu.make_async_copy(z_hbm, z_ref, loc_sem.at[4])
    load_z.start()
    for half in range(TOK // HD):
        kvs[pl.ds(half * HD, HD), pl.ds(HD, HD)] = v_ref[pl.ds(half * HD, HD), :].T

    halves = TOK // LANE
    goal = lax.shift_right_logical(dest_ref[pl.ds(me * halves, halves), :], TOK_BITS) * RUN
    goal = goal + lax.broadcasted_iota(jnp.int32, (halves, LANE), 1) % RUN
    slot = lax.broadcasted_iota(jnp.int32, (TOK, LANE), 0)
    choice = jnp.concatenate(
        [jnp.where(slot == goal[i : i + 1], 1.0, 0.0) for i in range(halves)], axis=1
    )
    staged = jnp.dot(choice.astype(BF16), q_ref[...], preferred_element_type=F32)
    qs[...] = staged.astype(BF16).reshape(NSEQ, RUN, CH)

    starts = doc_starts(len_ref)
    token = anchor + lax.broadcasted_iota(jnp.int32, (TOK, LANE), 0)
    depth = token - start_of(token, starts)

    def convolve(count, cols, far):
        total = cb_ref[:, cols] + cw_ref[pl.ds(0, 1), cols] * ext[pl.ds(8, count), cols]
        for lag in range(1, TAPS):
            window = ext[pl.ds(8 - lag, count), cols]
            total = total + cw_ref[pl.ds(lag, 1), cols] * jnp.where(far >= lag, window, 0.0)
        inner[pl.ds(0, count), cols] = silu(total).astype(BF16)

    def conv_columns(i, carry):
        cols = pl.ds(pl.multiple_of(i * LANE, LANE), LANE)
        ext[pl.ds(0, 8), cols] = jnp.zeros((8, LANE), F32)
        ext[pl.ds(8, TOK), cols] = x_ref[:, cols].astype(F32)
        convolve(TOK, cols, depth)
        return carry

    lax.fori_loop(0, SUB, conv_columns, 0)
    load_k.wait()
    pl.semaphore_wait(barrier, NSEQ - 1 + NZ - 1)

    def remote(src, dst, send, recv, device):
        return pltpu.make_async_remote_copy(
            src_ref=src,
            dst_ref=dst,
            send_sem=send,
            recv_sem=recv,
            device_id=device,
            device_id_type=MESH,
        )

    def offset(a, b, core):
        a, b = a % NX, b % NY
        return (
            lax.rem(x + a * (1 - core) + b * core, NX),
            lax.rem(y + a * core + b * (1 - core), NY),
        )

    def rows_of(a, b, core):
        px, py = offset(a, b, core)
        return pl.ds(pl.multiple_of(((px * NY + py) * NC + core) * TOK, TOK), TOK)

    partner = (x, y, 1 - c, z)
    after = lax.rem(me + 1, NSEQ)
    halo_copy = remote(
        x_ref.at[pl.ds(TOK - 16, 16)], halo, halo_sem.at[0], halo_sem.at[1], seq_device(after, z)
    )
    halo_copy.start()
    mine = kv_out.at[rows_of(0, 0, c)]
    sends = []
    for a in range(1, NX):
        px, py = offset(a, 0, c)
        copy = remote(kvs, mine, kv_send.at[a], kv_recv.at[a], (px, py, c, z))
        copy.start()
        sends.append(copy)
    copy = remote(kvs, mine, kv_send.at[16], kv_recv.at[16], partner)
    copy.start()
    sends.append(copy)
    keep_kv = pltpu.make_async_copy(kvs, mine, loc_sem.at[0])
    keep_kv.start()
    q_rows = pl.ds(pl.multiple_of(me * RUN, RUN), RUN)
    for k in range(1, NSEQ):
        j = lax.rem(me + k, NSEQ)
        copy = remote(qs.at[j], q_out.at[q_rows], q_send.at[k], q_recv.at[k], seq_device(j, z))
        copy.start()
        sends.append(copy)
    keep_q = pltpu.make_async_copy(qs.at[me], q_out.at[q_rows], loc_sem.at[1])
    keep_q.start()

    halo_copy.wait()
    ext[pl.ds(0, 8), :] = halo[pl.ds(8, 8), :].astype(F32)
    near = anchor + lax.broadcasted_iota(jnp.int32, (16, CH), 0)
    convolve(16, pl.ds(0, CH), near - start_of(near, starts))

    load_x.wait()
    partial = lax.dot_general(
        inner[...], xw_ref[...], (((1,), (1,)), ((), ())), preferred_element_type=F32
    ).astype(BF16)
    slice_rows = TOK // NZ
    part[...] = partial.reshape(NZ, slice_rows, PROJ)
    up = (x, y, c, lax.rem(z + 1, NZ))
    down = (x, y, c, lax.rem(z + NZ - 1, NZ))

    def ring_plus(s):
        src = part.at[lax.rem(z + 4, NZ)] if s == 1 else go_plus.at[s]
        return remote(src, rs_plus.at[s], rs_send.at[s], rs_recv.at[s], up)

    def ring_minus(s):
        src = part.at[lax.rem(z + 5, NZ)] if s == 1 else go_minus.at[s]
        return remote(src, rs_minus.at[s], rs_send.at[4 + s], rs_recv.at[4 + s], down)

    plus, minus = ring_plus(1), ring_minus(1)
    plus.start()
    minus.start()
    sends += [plus, minus]

    def wait_kv(slot_rows, index):
        remote(kvs, kv_out.at[slot_rows], kv_send.at[0], kv_recv.at[index], partner).wait_recv()

    for s in range(1, 4):
        plus.wait_recv()
        go_plus[s + 1] = (rs_plus[s].astype(F32) + part[lax.rem(z + 4 - s, NZ)].astype(F32)).astype(BF16)
        plus = ring_plus(s + 1)
        plus.start()
        sends.append(plus)
        minus.wait_recv()
        if s < 3:
            go_minus[s + 1] = (
                rs_minus[s].astype(F32) + part[lax.rem(z + 5 + s, NZ)].astype(F32)
            ).astype(BF16)
            minus = ring_minus(s + 1)
            minus.start()
            sends.append(minus)
        if s == 1:
            for a in range(NX):
                if a > 0:
                    wait_kv(rows_of(-a, 0, c), a)
                block = kv_out.at[rows_of(-a, 0, c)] if a > 0 else kvs
                target = kv_out.at[rows_of(-a, 0, c)]
                for b in range(1, NY):
                    px, py = offset(0, b, c)
                    index = b * NX + a
                    copy = remote(
                        block, target, kv_send.at[index], kv_recv.at[index], (px, py, c, z)
                    )
                    copy.start()
                    sends.append(copy)
                if a > 0:
                    copy = remote(
                        block, target, kv_send.at[16 + a], kv_recv.at[16 + a], partner
                    )
                    copy.start()
                    sends.append(copy)
    plus.wait_recv()
    total = part[z].astype(F32) + rs_plus[4].astype(F32) + rs_minus[3].astype(F32)

    def proj_rows(chunk):
        return pl.ds(pl.multiple_of(lax.rem(chunk, NZ) * slice_rows, slice_rows), slice_rows)

    proj[proj_rows(z), :] = total.astype(BF16)

    def pass_plus(s):
        rows = proj.at[proj_rows(z + NZ + 1 - s)]
        return remote(rows, rows, ag_send.at[s], ag_recv.at[s], up)

    def pass_minus(s):
        rows = proj.at[proj_rows(z + s - 1)]
        return remote(rows, rows, ag_send.at[4 + s], ag_recv.at[4 + s], down)

    def got_plus(s):
        rows = proj.at[proj_rows(z + NZ - s)]
        remote(rows, rows, ag_send.at[s], ag_recv.at[s], up).wait_recv()

    def got_minus(s):
        rows = proj.at[proj_rows(z + s)]
        remote(rows, rows, ag_send.at[4 + s], ag_recv.at[4 + s], down).wait_recv()

    for s in range(1, 5):
        if s > 1:
            got_plus(s - 1)
        copy = pass_plus(s)
        copy.start()
        sends.append(copy)
        if s < 4:
            if s > 1:
                got_minus(s - 1)
            copy = pass_minus(s)
            copy.start()
            sends.append(copy)
    spots = (TOKENS // LANE, LANE)
    spot = lax.broadcasted_iota(jnp.int32, spots, 1)
    ours = (lax.shift_right_logical(dest_ref[...], TOK_BITS) == me) & (spot % RUN == 0)
    spot = spot + LANE * lax.broadcasted_iota(jnp.int32, spots, 0)
    found = jnp.sum(jnp.where(ours, spot, 0).astype(F32), axis=1, keepdims=True)
    pos_out[...] = jnp.broadcast_to(found, spots).astype(jnp.int32)
    for j in range(SUB):
        cols = pl.ds(j * LANE, LANE)
        rates[pl.ds(j, NS, stride=SUB), :] = rate_ref[:, cols] * (-LOG2E)
    got_minus(3)
    got_plus(4)

    load_d.wait()
    begins = depth == 0
    low = proj[:, pl.ds(0, RANK)]
    for j in range(SUB):
        cols = pl.ds(j * LANE, LANE)
        if j % 2 == 0:
            both = pl.ds(j * LANE, 2 * LANE)
            raw = jnp.dot(low, dtw_ref[:, both], preferred_element_type=F32)
        value = raw[:, j % 2 * LANE : (j % 2 + 1) * LANE] + dtb_ref[:, cols]
        fade = jnp.exp2(jnp.abs(value) * (-LOG2E))
        series = fade - (0.5 * fade) * fade
        tail = jnp.where(fade < 1.0e-3, series, jnp.log(1.0 + fade))
        step = jnp.maximum(value, 0.0) + tail
        drives[pl.ds(j, TOK, stride=SUB), :] = step * inner[:, cols].astype(F32)
        step = jnp.where(begins, BIG_STEP, step)
        sums[pl.ds(j, 1), :] = jnp.sum(step, axis=0, keepdims=True)
        steps[pl.ds(j, TOK, stride=SUB), :] = step

    def widen(first):
        row = lax.broadcasted_iota(jnp.int32, (2 * NS, NS * LANE), 0)
        col = lax.broadcasted_iota(jnp.int32, (2 * NS, NS * LANE), 1)
        pick = jnp.where(lax.div(col, LANE) + first == row, 1.0, 0.0).astype(BF16)
        wide = jnp.dot(proj[:, pl.ds(RANK, 2 * NS)], pick, preferred_element_type=F32)
        for n in range(NS):
            spread[pl.ds((first + n) * TOK, TOK), :] = wide[:, n * LANE : (n + 1) * LANE]

    widen(0)
    rate = [rates[pl.ds(n * SUB, SUB), :] for n in range(NS)]

    def advance(t, carried):
        rows = pl.ds(pl.multiple_of(t * SUB, SUB), SUB)
        step = steps[rows, :]
        drive = drives[rows, :]
        result = []
        for n in range(NS):
            b = spread[pl.ds(n * TOK + t, SUB, stride=0), :]
            decay = jnp.exp2(step * rate[n])
            decays[t, pl.ds(n * SUB, SUB), :] = decay
            result.append(decay * carried[n] + b * drive)
        return tuple(result)

    zero = jnp.zeros((SUB, LANE), F32)
    state = lax.fori_loop(0, TOK, advance, (zero,) * NS, unroll=4)

    def pack(into, states, total):
        for n in range(0, NS, 2):
            pair = jnp.concatenate([states[n], states[n + 1]], axis=0)
            into[pl.ds(n * SUB, 2 * SUB), :] = pair.astype(BF16)
        high = total.astype(BF16).astype(F32)
        pair = jnp.concatenate([high, total - high], axis=0)
        into[pl.ds(NS * SUB, 2 * SUB), :] = pair.astype(BF16)

    def unpack(taken):
        block = taken[...].astype(F32).reshape(NS + 2, SUB, LANE)
        return [block[n] for n in range(NS)], block[NS] + block[NS + 1]

    def follow(states, block, total, passed=None):
        result = []
        for n in range(NS):
            moved = jnp.exp2(rate[n] * total) * states[n] + block[n]
            result.append(moved if passed is None else jnp.where(passed, moved, states[n]))
        return result

    pack(st_own, state, sums[...])
    pair_copy = remote(st_own, st_pair, st_send.at[0], st_recv.at[0], partner)
    pair_copy.start()
    sends.append(pair_copy)

    widen(NS)

    def local_token(t, carried):
        so_far, states = carried
        rows = pl.ds(pl.multiple_of(t * SUB, SUB), SUB)
        drive = drives[rows, :]
        passed = []
        result = []
        total = None
        for n in range(NS):
            decay = decays[t, pl.ds(n * SUB, SUB), :]
            b = spread[pl.ds(n * TOK + t, SUB, stride=0), :]
            weight = spread[pl.ds((NS + n) * TOK + t, SUB, stride=0), :]
            new = decay * states[n] + b * drive
            result.append(new)
            total = weight * new if total is None else total + weight * new
            left = so_far[n] * decay
            passed.append(left)
            gains[t, pl.ds(n * SUB, SUB), :] = weight * left
        ys[rows, :] = total
        return tuple(passed), tuple(result)

    carried = ((jnp.ones((SUB, LANE), F32),) * NS, (zero,) * NS)
    cuts = (0, 40, 144, TOK)
    carried = lax.fori_loop(cuts[0], cuts[1], local_token, carried, unroll=2)

    pair_copy.wait_recv()
    own_state, own_total = unpack(st_own)
    other_state, other_total = unpack(st_pair)
    first_core = c == 0
    early = [jnp.where(first_core, p, q) for p, q in zip(own_state, other_state)]
    late = [jnp.where(first_core, q, p) for p, q in zip(own_state, other_state)]
    late_total = jnp.where(first_core, other_total, own_total)
    chip_state = follow(early, late, late_total)
    pack(st_y.at[0], chip_state, own_total + other_total)
    level = []
    for k in range(1, NY):
        copy = remote(
            st_y.at[0], st_y.at[k], st_send.at[k], st_recv.at[k], (x, lax.rem(y + k, NY), c, z)
        )
        copy.start()
        level.append(copy)
    sends += level
    carried = lax.fori_loop(cuts[1], cuts[2], local_token, carried, unroll=2)

    for copy in level:
        copy.wait_recv()
    column, column_total = unpack(st_y.at[lax.rem(y + NY, NY)])
    for j in range(1, NY):
        block, total = unpack(st_y.at[lax.rem(y + NY - j, NY)])
        column = follow(column, block, total)
        column_total = column_total + total
    pack(st_x.at[0], column, column_total)
    level = []
    for k in range(1, NX):
        copy = remote(
            st_x.at[0], st_x.at[k], st_send.at[4 + k], st_recv.at[4 + k], (lax.rem(x + k, NX), y, c, z)
        )
        copy.start()
        level.append(copy)
    sends += level
    carried = lax.fori_loop(cuts[2], cuts[3], local_token, carried, unroll=2)

    for b in range(1, NY):
        for a in range(NX):
            index = b * NX + a
            wait_kv(rows_of(-a, -b, c), index)
            block = kv_out.at[rows_of(-a, -b, c)]
            copy = remote(block, block, kv_send.at[16 + index], kv_recv.at[16 + index], partner)
            copy.start()
            sends.append(copy)

    for copy in level:
        copy.wait_recv()
    entering = [zero] * NS
    for j in range(NX - 1):
        block, total = unpack(st_x.at[lax.rem(x + NX - j, NX)])
        entering = follow(entering, block, total, x > j)
    for j in range(NY - 1):
        block, total = unpack(st_y.at[lax.rem(y + NY - j, NY)])
        entering = follow(entering, block, total, y > j)
    entering = follow(entering, early, jnp.where(first_core, own_total, other_total), c > 0)

    def correct(t, carry):
        rows = pl.ds(pl.multiple_of(t * SUB, SUB), SUB)
        total = ys[rows, :]
        for n in range(NS):
            total = total + gains[t, pl.ds(n * SUB, SUB), :] * entering[n]
        ys[rows, :] = total
        return carry

    lax.fori_loop(0, TOK, correct, 0, unroll=4)
    load_z.wait()
    for j in range(SUB):
        cols = pl.ds(j * LANE, LANE)
        scanned = ys[pl.ds(j, TOK, stride=SUB), :]
        scanned = scanned + skip_ref[:, cols] * inner[:, cols].astype(F32)
        out[:, cols] = (scanned * silu(z_ref[:, cols].astype(F32))).astype(BF16)

    for k in range(1, NSEQ):
        rows = pl.ds(pl.multiple_of(lax.rem(me + NSEQ - k, NSEQ) * RUN, RUN), RUN)
        remote(qs.at[0], q_out.at[rows], q_send.at[k], q_recv.at[k], partner).wait_recv()
    for b in range(NY):
        for a in range(NX):
            wait_kv(rows_of(-a, -b, 1 - c), 16 + b * NX + a)
    for copy in sends:
        copy.wait_send()
    keep_kv.wait()
    keep_q.wait()


def mix(dest, lengths, q, k, v, x, z, cw, cb, xw, dtw, dtb, rate, skip):
    dma = pltpu.SemaphoreType.DMA
    states = ((NS + 2) * SUB, LANE)
    chunk = (TOK // NZ, PROJ)
    return pl.pallas_call(
        mixer_kernel,
        out_shape=(
            jax.ShapeDtypeStruct((TOK, CH), BF16),
            jax.ShapeDtypeStruct((NSEQ * TOK, 2 * HD), BF16),
            jax.ShapeDtypeStruct((TOKENS // LANE, LANE), jnp.int32),
            jax.ShapeDtypeStruct((TOK, CH), BF16),
        ),
        in_specs=[
            whole(),
            whole(pltpu.SMEM),
            whole(),
            whole(pl.ANY),
            whole(),
            whole(),
            whole(pl.ANY),
            whole(),
            whole(),
            whole(pl.ANY),
            whole(pl.ANY),
        ]
        + [whole()] * 3,
        out_specs=(whole(pl.ANY), whole(pl.ANY), whole(), whole()),
        scratch_shapes=[
            VM((TOK, 2 * HD), BF16),
            VM((NSEQ, RUN, CH), BF16),
            VM((16, CH), BF16),
            VM((TOK + 8, CH), F32),
            VM((TOK, CH), BF16),
            VM((NZ, *chunk), BF16),
            VM((5, *chunk), BF16),
            VM((4, *chunk), BF16),
            VM((5, *chunk), BF16),
            VM((4, *chunk), BF16),
            VM((TOK, PROJ), BF16),
            VM((TOK * SUB, LANE), F32),
            VM((TOK * SUB, LANE), F32),
            VM((NS * SUB, LANE), F32),
            VM((2 * NS * TOK, LANE), F32),
            VM((TOK, NS * SUB, LANE), F32),
            VM((TOK * SUB, LANE), F32),
            VM((SUB, LANE), F32),
            VM(states, BF16),
            VM(states, BF16),
            VM((NY, *states), BF16),
            VM((NX, *states), BF16),
            VM((TOK, NS * SUB, LANE), F32),
            VM((TOK, CH), BF16),
            VM((PROJ, CH), BF16),
            VM((RANK, CH), BF16),
            dma((5,)),
            dma((2,)),
            dma((32,)),
            dma((32,)),
            dma((NSEQ,)),
            dma((NSEQ,)),
            dma((NZ,)),
            dma((NZ,)),
            dma((NZ,)),
            dma((NZ,)),
            dma((NZ,)),
            dma((NZ,)),
        ],
        compiler_params=pltpu.CompilerParams(
            collective_id=0, has_side_effects=True, vmem_limit_bytes=VLIM
        ),
        name="mixer",
    )(dest, lengths, q, k, v, x, z, cw, cb, xw, dtw, dtb, rate, skip)


def attend_kernel(pos_ref, len_ref, q_ref, kv_ref, out, scores_a, scores_b):
    g = pl.program_id(0)
    heads = CH // HD
    rows = GROUP * RUN
    count = heads * rows
    wide = 2 * BK
    per = TOK * GROUP // wide
    starts = doc_starts(len_ref)
    halves = TOK // LANE
    bases = [
        sum(pos_ref[(g * GROUP + i) * halves + j, 0] for j in range(halves)) for i in range(GROUP)
    ]
    lane = lax.broadcasted_iota(jnp.int32, (1, LANE), 1) % rows
    base = bases[0]
    for i in range(1, GROUP):
        base = jnp.where(lane >= i * RUN, bases[i], base)
    pos = base + lane % RUN
    start = start_of(pos, starts)
    top = g * per
    first = jnp.minimum(start_of(bases[0], starts) // wide, top)
    last_start = start_of(bases[GROUP - 1] + RUN - 1, starts)
    plain = jnp.maximum(jnp.minimum((last_start + wide - 1) // wide, top), first)
    q = jnp.concatenate([q_ref[:, h * HD : (h + 1) * HD] for h in range(heads)], axis=0)
    scale = HD**-0.5 * LOG2E
    key_row = lax.broadcasted_iota(jnp.int32, (BK, LANE), 0)
    ones = jnp.ones((16, BK), BF16)

    def score(into, i):
        keys = kv_ref[pl.ds(pl.multiple_of(i * BK, BK), BK), pl.ds(0, HD)]
        into[...] = lax.dot_general(
            keys, q, (((1,), (1,)), ((), ())), preferred_element_type=F32
        )

    def absorb(taken, i, carried, masked):
        begin = pl.multiple_of(i * BK, BK)
        best, summed = carried
        scores = taken[...]
        if masked:
            visible = (key_row <= pos - begin) & (key_row >= start - begin)
            scores = jnp.concatenate(
                [
                    jnp.where(visible, scores[:, j : j + LANE], MASKED)
                    for j in range(0, count, LANE)
                ],
                axis=1,
            )
        new_best = jnp.maximum(best, jnp.max(scores, axis=0, keepdims=True) * scale)
        weights = jnp.exp2(scores * scale - new_best).astype(BF16)
        rescale = jnp.exp2(best - new_best)
        values = jnp.concatenate(
            [kv_ref[pl.ds(begin + j, HD), pl.ds(HD, HD)] for j in range(0, BK, HD)], axis=1
        )
        values = jnp.concatenate([values, ones], axis=0)
        product = jnp.dot(values, weights, preferred_element_type=F32)
        return new_best, summed * rescale + product

    def pair(i, carried, masked, more=True):
        score(scores_b, 2 * i + 1)
        carried = absorb(scores_a, 2 * i, carried, masked)
        if more:
            score(scores_a, 2 * i + 2)
        return absorb(scores_b, 2 * i + 1, carried, masked)

    carried = (jnp.full((1, count), MASKED * scale, F32), jnp.zeros((HD + 16, count), F32))
    score(scores_a, 2 * first)
    carried = lax.fori_loop(first, plain, lambda i, v: pair(i, v, True), carried)
    carried = lax.fori_loop(plain, top, lambda i, v: pair(i, v, False), carried)
    for i in range(per):
        carried = pair(top + i, carried, True, i < per - 1)
    summed = carried[1]
    result = (summed[:HD] / summed[HD : HD + 1]).T.astype(BF16)
    for h in range(heads):
        out[:, h * HD : (h + 1) * HD] = result[h * rows : (h + 1) * rows]


def attend(positions, lengths, q, kv):
    rows = GROUP * RUN
    return pl.pallas_call(
        attend_kernel,
        out_shape=jax.ShapeDtypeStruct((TOK, CH), BF16),
        grid=(NSEQ // GROUP,),
        in_specs=[
            whole(pltpu.SMEM),
            whole(pltpu.SMEM),
            pl.BlockSpec((rows, CH), lambda g: (g, 0)),
            whole(),
        ],
        out_specs=pl.BlockSpec((rows, CH), lambda g: (g, 0)),
        scratch_shapes=[VM((BK, CH // HD * rows), F32)] * 2,
        compiler_params=pltpu.CompilerParams(vmem_limit_bytes=VLIM),
        name="attend",
    )(positions, lengths, q, kv)


def local(
    x_branch,
    z_branch,
    conv_weight,
    conv_bias,
    xproj_weight,
    dt_weight,
    dt_bias,
    decay_rate,
    skip_gain,
    query_rows,
    key_rows,
    value_rows,
    lengths,
    destination,
):
    q, kv, positions, mamba_out = mix(
        destination.reshape(TOKENS // LANE, LANE),
        lengths,
        query_rows,
        key_rows,
        value_rows,
        x_branch,
        z_branch,
        conv_weight,
        conv_bias.reshape(1, CH),
        xproj_weight.T,
        dt_weight,
        dt_bias.reshape(1, CH),
        decay_rate,
        skip_gain.reshape(1, CH),
    )
    regrouped = attend(positions, lengths, q, kv)
    return (mamba_out, regrouped)


def solution(mesh):
    torus = Mesh(mesh.devices.reshape(NX, NY, NC, mesh.shape["mp"]), (*SEQ, "mp"))
    in_specs = (
        P(SEQ, "mp"),
        P(SEQ, "mp"),
        P(None, "mp"),
        P("mp"),
        P("mp", None),
        P(None, "mp"),
        P("mp"),
        P(None, "mp"),
        P("mp"),
        P(SEQ, "mp"),
        P(SEQ, "mp"),
        P(SEQ, "mp"),
        P(),
        P(),
    )
    out_specs = (P(SEQ, "mp"), P(SEQ, "mp"))
    return jax.shard_map(local, mesh=torus, in_specs=in_specs, out_specs=out_specs, check_vma=False)
```

profile of v0, /device:TPU:1, one launch (start us, length us, event | category | flops | bytes accessed | tf_op | source)
XLA Modules:
  0.0 77.4 jit_solution(5780632299734868315)
XLA Ops:
  0.6 60.4 %mixer.1 = (bf16[256,1024]{1,0:T(8,128)(2,1)}, bf16[8192,256]{1,0:T(8,128)(2,1)}, s32[64,128]{1,0:T(8,128)}, bf16[256,1024]{1,0:T(8,128)(2,1)}) custom-call(s32[64,128]{1,0:T(8,128)} %bitcast.6, s32[4]{0:T(128)} %len_ref.3, bf16[256,1024]{1,0:T(8,128)(2,1)} %q_ref.1, bf16[256,128]{1,0:T(8,128)(2,1)} %k_ref.1, bf16[256,128]{1,0:T(8,128)(2,1)} %v_ref.1, ...), custom_call_target="tpu_custom_call" | custom-call | tf_op jit(solution)/shard_map/mixer/pallas_call | solution.py:528
  61.0 0.0 copy-start
  61.1 15.6 %attend.1 = bf16[256,1024]{1,0:T(8,128)(2,1)} custom-call(s32[64,128]{1,0:T(8,128)} %get-tuple-element.7.pos_ref, s32[4]{0:T(128)} %len_ref.3, bf16[256,1024]{1,0:T(8,128)(2,1)} %get-tuple-element.8.q_ref, bf16[8192,256]{1,0:T(8,128)(2,1)} %get-tuple-element.9.kv_ref), custom_call_target="tpu_custom_call" | custom-call | tf_op jit(solution)/shard_map/attend/pallas_call | solution.py:675
  76.6 0.0 copy-done
  76.6 0.8 %copy.17 = bf16[256,1024]{1,0:T(8,128)(2,1)} copy(bf16[256,1024]{1,0:T(8,128)(2,1)S(1)} %copy-done) | data formatting | bytes 1048576
Async XLA Ops:
  61.0 15.6 %copy-start = (bf16[256,1024]{1,0:T(8,128)(2,1)S(1)}, bf16[256,1024]{1,0:T(8,128)(2,1)}, u32[]{:S(2)}) copy-start(bf16[256,1024]{1,0:T(8,128)(2,1)} %get-tuple-element.12) | copy-start | bytes 1572868
where the time goes:
time: 77.5 us; the launch traced here: 77.4 us
  Pallas kernels  76 us (98%)
  local copies, waits for them, and re-layouts  0.8 us (1%)
    pallas_call x1, Pallas kernels, mix(): pl.pallas_call(mixer_kernel, out_shape=(jax.ShapeDtypeStruct((TOK, CH), B...  60.4 us
    pallas_call x1, Pallas kernels, attend(): pl.pallas_call(attend_kernel, out_shape=jax.ShapeDtypeStruct((TOK, CH), B...  15.6 us

commit v1 on v0

--- a/solution.py
+++ b/solution.py
@@ -27,6 +27,7 @@
 PROJ = RANK + 2 * NS
 HD = 128
 TAPS = 4
+HALVES = 2
 BIG_STEP = 1.0e7
 MASKED = -1.0e30
 GROUP = 8
@@ -111,6 +112,7 @@
     st_y,
     st_x,
     decays,
+    gates,
     z_ref,
     xw_ref,
     dtw_ref,
@@ -147,6 +149,54 @@
     load_d.start()
     load_z = pltpu.make_async_copy(z_hbm, z_ref, loc_sem.at[4])
     load_z.start()
+    starts = doc_starts(len_ref)
+    token = anchor + lax.broadcasted_iota(jnp.int32, (TOK, LANE), 0)
+    depth = token - start_of(token, starts)
+
+    def convolve(count, cols, far):
+        total = cb_ref[:, cols] + cw_ref[pl.ds(0, 1), cols] * ext[pl.ds(8, count), cols]
+        for lag in range(1, TAPS):
+            window = ext[pl.ds(8 - lag, count), cols]
+            total = total + cw_ref[pl.ds(lag, 1), cols] * jnp.where(far >= lag, window, 0.0)
+        inner[pl.ds(0, count), cols] = silu(total).astype(BF16)
+
+    def conv_columns(i, carry):
+        cols = pl.ds(pl.multiple_of(i * LANE, LANE), LANE)
+        ext[pl.ds(0, 8), cols] = jnp.zeros((8, LANE), F32)
+        ext[pl.ds(8, TOK), cols] = x_ref[:, cols].astype(F32)
+        convolve(TOK, cols, depth)
+        return carry
+
+    lax.fori_loop(0, SUB, conv_columns, 0)
+    pl.semaphore_wait(barrier, NSEQ - 1 + NZ - 1)
+
+    def remote(src, dst, send, recv, device):
+        return pltpu.make_async_remote_copy(
+            src_ref=src,
+            dst_ref=dst,
+            send_sem=send,
+            recv_sem=recv,
+            device_id=device,
+            device_id_type=MESH,
+        )
+
+    def offset(a, b, core):
+        a, b = a % NX, b % NY
+        return (
+            lax.rem(x + a * (1 - core) + b * core, NX),
+            lax.rem(y + a * core + b * (1 - core), NY),
+        )
+
+    def rows_of(a, b, core):
+        px, py = offset(a, b, core)
+        return pl.ds(pl.multiple_of(((px * NY + py) * NC + core) * TOK, TOK), TOK)
+
+    partner = (x, y, 1 - c, z)
+    after = lax.rem(me + 1, NSEQ)
+    halo_copy = remote(
+        x_ref.at[pl.ds(TOK - 16, 16)], halo, halo_sem.at[0], halo_sem.at[1], seq_device(after, z)
+    )
+    halo_copy.start()
     for half in range(TOK // HD):
         kvs[pl.ds(half * HD, HD), pl.ds(HD, HD)] = v_ref[pl.ds(half * HD, HD), :].T
 
@@ -159,56 +209,7 @@
     )
     staged = jnp.dot(choice.astype(BF16), q_ref[...], preferred_element_type=F32)
     qs[...] = staged.astype(BF16).reshape(NSEQ, RUN, CH)
-
-    starts = doc_starts(len_ref)
-    token = anchor + lax.broadcasted_iota(jnp.int32, (TOK, LANE), 0)
-    depth = token - start_of(token, starts)
-
-    def convolve(count, cols, far):
-        total = cb_ref[:, cols] + cw_ref[pl.ds(0, 1), cols] * ext[pl.ds(8, count), cols]
-        for lag in range(1, TAPS):
-            window = ext[pl.ds(8 - lag, count), cols]
-            total = total + cw_ref[pl.ds(lag, 1), cols] * jnp.where(far >= lag, window, 0.0)
-        inner[pl.ds(0, count), cols] = silu(total).astype(BF16)
-
-    def conv_columns(i, carry):
-        cols = pl.ds(pl.multiple_of(i * LANE, LANE), LANE)
-        ext[pl.ds(0, 8), cols] = jnp.zeros((8, LANE), F32)
-        ext[pl.ds(8, TOK), cols] = x_ref[:, cols].astype(F32)
-        convolve(TOK, cols, depth)
-        return carry
-
-    lax.fori_loop(0, SUB, conv_columns, 0)
     load_k.wait()
-    pl.semaphore_wait(barrier, NSEQ - 1 + NZ - 1)
-
-    def remote(src, dst, send, recv, device):
-        return pltpu.make_async_remote_copy(
-            src_ref=src,
-            dst_ref=dst,
-            send_sem=send,
-            recv_sem=recv,
-            device_id=device,
-            device_id_type=MESH,
-        )
-
-    def offset(a, b, core):
-        a, b = a % NX, b % NY
-        return (
-            lax.rem(x + a * (1 - core) + b * core, NX),
-            lax.rem(y + a * core + b * (1 - core), NY),
-        )
-
-    def rows_of(a, b, core):
-        px, py = offset(a, b, core)
-        return pl.ds(pl.multiple_of(((px * NY + py) * NC + core) * TOK, TOK), TOK)
-
-    partner = (x, y, 1 - c, z)
-    after = lax.rem(me + 1, NSEQ)
-    halo_copy = remote(
-        x_ref.at[pl.ds(TOK - 16, 16)], halo, halo_sem.at[0], halo_sem.at[1], seq_device(after, z)
-    )
-    halo_copy.start()
     mine = kv_out.at[rows_of(0, 0, c)]
     sends = []
     for a in range(1, NX):
@@ -240,41 +241,46 @@
         inner[...], xw_ref[...], (((1,), (1,)), ((), ())), preferred_element_type=F32
     ).astype(BF16)
     slice_rows = TOK // NZ
-    part[...] = partial.reshape(NZ, slice_rows, PROJ)
+    part_rows = slice_rows // HALVES
+    part[...] = partial.reshape(NZ, HALVES, part_rows, PROJ)
     up = (x, y, c, lax.rem(z + 1, NZ))
     down = (x, y, c, lax.rem(z + NZ - 1, NZ))
 
-    def ring_plus(s):
-        src = part.at[lax.rem(z + 4, NZ)] if s == 1 else go_plus.at[s]
-        return remote(src, rs_plus.at[s], rs_send.at[s], rs_recv.at[s], up)
-
-    def ring_minus(s):
-        src = part.at[lax.rem(z + 5, NZ)] if s == 1 else go_minus.at[s]
-        return remote(src, rs_minus.at[s], rs_send.at[4 + s], rs_recv.at[4 + s], down)
-
-    plus, minus = ring_plus(1), ring_minus(1)
-    plus.start()
-    minus.start()
-    sends += [plus, minus]
+    def ring_plus(s, h):
+        src = part.at[lax.rem(z + 4, NZ), h] if s == 1 else go_plus.at[s, h]
+        index = h * NZ + s
+        return remote(src, rs_plus.at[s, h], rs_send.at[index], rs_recv.at[index], up)
+
+    def ring_minus(s, h):
+        src = part.at[lax.rem(z + 5, NZ), h] if s == 1 else go_minus.at[s, h]
+        index = h * NZ + 4 + s
+        return remote(src, rs_minus.at[s, h], rs_send.at[index], rs_recv.at[index], down)
+
+    def begin(copy):
+        copy.start()
+        sends.append(copy)
+        return copy
+
+    plus, minus = [], []
+    for h in range(HALVES):
+        plus.append(begin(ring_plus(1, h)))
+        minus.append(begin(ring_minus(1, h)))
 
     def wait_kv(slot_rows, index):
         remote(kvs, kv_out.at[slot_rows], kv_send.at[0], kv_recv.at[index], partner).wait_recv()
 
     for s in range(1, 4):
-        plus.wait_recv()
-        go_plus[s + 1] = (rs_plus[s].astype(F32) + part[lax.rem(z + 4 - s, NZ)].astype(F32)).astype(BF16)
-        plus = ring_plus(s + 1)
-        plus.start()
-        sends.append(plus)
-        minus.wait_recv()
-        if s < 3:
-            go_minus[s + 1] = (
-                rs_minus[s].astype(F32) + part[lax.rem(z + 5 + s, NZ)].astype(F32)
-            ).astype(BF16)
-            minus = ring_minus(s + 1)
-            minus.start()
-            sends.append(minus)
-        if s == 1:
+        for h in range(HALVES):
+            plus[h].wait_recv()
+            ours = part[lax.rem(z + 4 - s, NZ), h].astype(F32)
+            go_plus[s + 1, h] = (rs_plus[s, h].astype(F32) + ours).astype(BF16)
+            plus[h] = begin(ring_plus(s + 1, h))
+            minus[h].wait_recv()
+            if s < 3:
+                ours = part[lax.rem(z + 5 + s, NZ), h].astype(F32)
+                go_minus[s + 1, h] = (rs_minus[s, h].astype(F32) + ours).astype(BF16)
+                minus[h] = begin(ring_minus(s + 1, h))
+        if s == 2:
             for a in range(NX):
                 if a > 0:
                     wait_kv(rows_of(-a, 0, c), a)
@@ -294,42 +300,44 @@
                     )
                     copy.start()
                     sends.append(copy)
-    plus.wait_recv()
-    total = part[z].astype(F32) + rs_plus[4].astype(F32) + rs_minus[3].astype(F32)
-
-    def proj_rows(chunk):
-        return pl.ds(pl.multiple_of(lax.rem(chunk, NZ) * slice_rows, slice_rows), slice_rows)
-
-    proj[proj_rows(z), :] = total.astype(BF16)
-
-    def pass_plus(s):
-        rows = proj.at[proj_rows(z + NZ + 1 - s)]
-        return remote(rows, rows, ag_send.at[s], ag_recv.at[s], up)
-
-    def pass_minus(s):
-        rows = proj.at[proj_rows(z + s - 1)]
-        return remote(rows, rows, ag_send.at[4 + s], ag_recv.at[4 + s], down)
-
-    def got_plus(s):
-        rows = proj.at[proj_rows(z + NZ - s)]
-        remote(rows, rows, ag_send.at[s], ag_recv.at[s], up).wait_recv()
-
-    def got_minus(s):
-        rows = proj.at[proj_rows(z + s)]
-        remote(rows, rows, ag_send.at[4 + s], ag_recv.at[4 + s], down).wait_recv()
-
-    for s in range(1, 5):
-        if s > 1:
-            got_plus(s - 1)
-        copy = pass_plus(s)
-        copy.start()
-        sends.append(copy)
-        if s < 4:
-            if s > 1:
-                got_minus(s - 1)
-            copy = pass_minus(s)
-            copy.start()
-            sends.append(copy)
+
+    def proj_rows(chunk, h):
+        first = lax.rem(chunk, NZ) * slice_rows + h * part_rows
+        return pl.ds(pl.multiple_of(first, part_rows), part_rows)
+
+    def pass_plus(s, h):
+        rows = proj.at[proj_rows(z + NZ + 1 - s, h)]
+        index = h * NZ + s
+        return remote(rows, rows, ag_send.at[index], ag_recv.at[index], up)
+
+    def pass_minus(s, h):
+        rows = proj.at[proj_rows(z + s - 1, h)]
+        index = h * NZ + 4 + s
+        return remote(rows, rows, ag_send.at[index], ag_recv.at[index], down)
+
+    def got_plus(s, h):
+        rows = proj.at[proj_rows(z + NZ - s, h)]
+        index = h * NZ + s
+        remote(rows, rows, ag_send.at[index], ag_recv.at[index], up).wait_recv()
+
+    def got_minus(s, h):
+        rows = proj.at[proj_rows(z + s, h)]
+        index = h * NZ + 4 + s
+        remote(rows, rows, ag_send.at[index], ag_recv.at[index], down).wait_recv()
+
+    for h in range(HALVES):
+        plus[h].wait_recv()
+        total = part[z, h].astype(F32) + rs_plus[4, h].astype(F32) + rs_minus[3, h].astype(F32)
+        proj[proj_rows(z, h), :] = total.astype(BF16)
+        begin(pass_plus(1, h))
+        begin(pass_minus(1, h))
+    for s in range(2, 5):
+        for h in range(HALVES):
+            got_plus(s - 1, h)
+            begin(pass_plus(s, h))
+            if s < 4:
+                got_minus(s - 1, h)
+                begin(pass_minus(s, h))
     spots = (TOKENS // LANE, LANE)
     spot = lax.broadcasted_iota(jnp.int32, spots, 1)
     ours = (lax.shift_right_logical(dest_ref[...], TOK_BITS) == me) & (spot % RUN == 0)
@@ -339,8 +347,9 @@
     for j in range(SUB):
         cols = pl.ds(j * LANE, LANE)
         rates[pl.ds(j, NS, stride=SUB), :] = rate_ref[:, cols] * (-LOG2E)
-    got_minus(3)
-    got_plus(4)
+    for h in range(HALVES):
+        got_minus(3, h)
+        got_plus(4, h)
 
     load_d.wait()
     begins = depth == 0
@@ -482,6 +491,13 @@
             copy.start()
             sends.append(copy)
 
+    load_z.wait()
+    for j in range(SUB):
+        cols = pl.ds(j * LANE, LANE)
+        gates[:, cols] = silu(z_ref[:, cols].astype(F32))
+        inner_gain = skip_ref[:, cols] * inner[:, cols].astype(F32)
+        kept = ys[pl.ds(j, TOK, stride=SUB), :]
+        ys[pl.ds(j, TOK, stride=SUB), :] = kept + inner_gain
     for copy in level:
         copy.wait_recv()
     entering = [zero] * NS
@@ -502,12 +518,9 @@
         return carry
 
     lax.fori_loop(0, TOK, correct, 0, unroll=4)
-    load_z.wait()
     for j in range(SUB):
         cols = pl.ds(j * LANE, LANE)
-        scanned = ys[pl.ds(j, TOK, stride=SUB), :]
-        scanned = scanned + skip_ref[:, cols] * inner[:, cols].astype(F32)
-        out[:, cols] = (scanned * silu(z_ref[:, cols].astype(F32))).astype(BF16)
+        out[:, cols] = (ys[pl.ds(j, TOK, stride=SUB), :] * gates[:, cols]).astype(BF16)
 
     for k in range(1, NSEQ):
         rows = pl.ds(pl.multiple_of(lax.rem(me + NSEQ - k, NSEQ) * RUN, RUN), RUN)
@@ -524,7 +537,7 @@
 def mix(dest, lengths, q, k, v, x, z, cw, cb, xw, dtw, dtb, rate, skip):
     dma = pltpu.SemaphoreType.DMA
     states = ((NS + 2) * SUB, LANE)
-    chunk = (TOK // NZ, PROJ)
+    chunk = (HALVES, TOK // NZ // HALVES, PROJ)
     return pl.pallas_call(
         mixer_kernel,
         out_shape=(
@@ -572,6 +585,7 @@
             VM((NY, *states), BF16),
             VM((NX, *states), BF16),
             VM((TOK, NS * SUB, LANE), F32),
+            VM((TOK, CH), F32),
             VM((TOK, CH), BF16),
             VM((PROJ, CH), BF16),
             VM((RANK, CH), BF16),
@@ -581,10 +595,10 @@
             dma((32,)),
             dma((NSEQ,)),
             dma((NSEQ,)),
-            dma((NZ,)),
-            dma((NZ,)),
-            dma((NZ,)),
-            dma((NZ,)),
+            dma((HALVES * NZ,)),
+            dma((HALVES * NZ,)),
+            dma((HALVES * NZ,)),
+            dma((HALVES * NZ,)),
             dma((NZ,)),
             dma((NZ,)),
         ],
@@ -595,49 +609,72 @@
     )(dest, lengths, q, k, v, x, z, cw, cb, xw, dtw, dtb, rate, skip)
 
 
-def attend_kernel(pos_ref, len_ref, q_ref, kv_ref, out, scores_a, scores_b):
+def attend_kernel(pos_ref, len_ref, q_ref, kv_hbm, out, scores_a, scores_b, kv_ref, sems):
     g = pl.program_id(0)
     heads = CH // HD
     rows = GROUP * RUN
     count = heads * rows
+    half = count // 2
+    half_rows = rows // 2
     wide = 2 * BK
-    per = TOK * GROUP // wide
+    span = TOK * GROUP
+    halves = TOK // LANE
+
+    def load(i):
+        part = pl.ds(pl.multiple_of(i * span, span), span)
+        return pltpu.make_async_copy(kv_hbm.at[part], kv_ref.at[part], sems.at[i])
+
+    @pl.when(g == 0)
+    def _():
+        for i in range(NSEQ // GROUP):
+            load(i).start()
+
     starts = doc_starts(len_ref)
-    halves = TOK // LANE
     bases = [
         sum(pos_ref[(g * GROUP + i) * halves + j, 0] for j in range(halves)) for i in range(GROUP)
     ]
-    lane = lax.broadcasted_iota(jnp.int32, (1, LANE), 1) % rows
-    base = bases[0]
-    for i in range(1, GROUP):
-        base = jnp.where(lane >= i * RUN, bases[i], base)
-    pos = base + lane % RUN
-    start = start_of(pos, starts)
-    top = g * per
-    first = jnp.minimum(start_of(bases[0], starts) // wide, top)
+    lane = lax.broadcasted_iota(jnp.int32, (1, LANE), 1) % half_rows
+
+    def lanes(firsts):
+        base = firsts[0]
+        for i in range(1, GROUP // 2):
+            base = jnp.where(lane >= i * RUN, firsts[i], base)
+        pos = base + lane % RUN
+        return pos, start_of(pos, starts)
+
+    bounds = (lanes(bases[: GROUP // 2]), lanes(bases[GROUP // 2 :]))
+    top = g * (span // wide)
+    first = jnp.minimum(lax.div(start_of(bases[0], starts), wide), top)
     last_start = start_of(bases[GROUP - 1] + RUN - 1, starts)
-    plain = jnp.maximum(jnp.minimum((last_start + wide - 1) // wide, top), first)
-    q = jnp.concatenate([q_ref[:, h * HD : (h + 1) * HD] for h in range(heads)], axis=0)
+    plain = jnp.maximum(jnp.minimum(lax.div(last_start + wide - 1, wide), top), first)
+    q = jnp.concatenate(
+        [
+            q_ref[i * half_rows : (i + 1) * half_rows, h * HD : (h + 1) * HD]
+            for i in range(2)
+            for h in range(heads)
+        ],
+        axis=0,
+    )
     scale = HD**-0.5 * LOG2E
     key_row = lax.broadcasted_iota(jnp.int32, (BK, LANE), 0)
     ones = jnp.ones((16, BK), BF16)
 
-    def score(into, i):
+    def score(into, i, low=0):
         keys = kv_ref[pl.ds(pl.multiple_of(i * BK, BK), BK), pl.ds(0, HD)]
-        into[...] = lax.dot_general(
-            keys, q, (((1,), (1,)), ((), ())), preferred_element_type=F32
+        into[:, low:count] = lax.dot_general(
+            keys, q[low:], (((1,), (1,)), ((), ())), preferred_element_type=F32
         )
 
-    def absorb(taken, i, carried, masked):
+    def absorb(taken, i, carried, masked, low=0):
         begin = pl.multiple_of(i * BK, BK)
         best, summed = carried
-        scores = taken[...]
+        scores = taken[:, low:count]
         if masked:
-            visible = (key_row <= pos - begin) & (key_row >= start - begin)
+            visible = [(key_row <= pos - begin) & (key_row >= at - begin) for pos, at in bounds]
             scores = jnp.concatenate(
                 [
-                    jnp.where(visible, scores[:, j : j + LANE], MASKED)
-                    for j in range(0, count, LANE)
+                    jnp.where(visible[(j + low) // half], scores[:, j : j + LANE], MASKED)
+                    for j in range(0, count - low, LANE)
                 ],
                 axis=1,
             )
@@ -651,23 +688,31 @@
         product = jnp.dot(values, weights, preferred_element_type=F32)
         return new_best, summed * rescale + product
 
-    def pair(i, carried, masked, more=True):
+    def pair(i, carried, masked):
         score(scores_b, 2 * i + 1)
         carried = absorb(scores_a, 2 * i, carried, masked)
-        if more:
-            score(scores_a, 2 * i + 2)
+        score(scores_a, 2 * i + 2)
         return absorb(scores_b, 2 * i + 1, carried, masked)
 
     carried = (jnp.full((1, count), MASKED * scale, F32), jnp.zeros((HD + 16, count), F32))
+    load(g).wait()
     score(scores_a, 2 * first)
     carried = lax.fori_loop(first, plain, lambda i, v: pair(i, v, True), carried)
     carried = lax.fori_loop(plain, top, lambda i, v: pair(i, v, False), carried)
-    for i in range(per):
-        carried = pair(top + i, carried, True, i < per - 1)
-    summed = carried[1]
-    result = (summed[:HD] / summed[HD : HD + 1]).T.astype(BF16)
-    for h in range(heads):
-        out[:, h * HD : (h + 1) * HD] = result[h * rows : (h + 1) * rows]
+    score(scores_b, 2 * top + 1)
+    carried = absorb(scores_a, 2 * top, carried, True)
+    score(scores_a, 2 * top + 2, half)
+    best, summed = absorb(scores_b, 2 * top + 1, carried, True)
+    later = (best[:, half:], summed[:, half:])
+    score(scores_b, 2 * top + 3, half)
+    later = absorb(scores_a, 2 * top + 2, later, True, half)
+    later = absorb(scores_b, 2 * top + 3, later, True, half)
+    for i, total in enumerate((summed[:, :half], later[1])):
+        result = (total[:HD] / total[HD : HD + 1]).T.astype(BF16)
+        for h in range(heads):
+            out[i * half_rows : (i + 1) * half_rows, h * HD : (h + 1) * HD] = result[
+                h * half_rows : (h + 1) * half_rows
+            ]
 
 
 def attend(positions, lengths, q, kv):
@@ -680,10 +725,11 @@
             whole(pltpu.SMEM),
             whole(pltpu.SMEM),
             pl.BlockSpec((rows, CH), lambda g: (g, 0)),
-            whole(),
+            whole(pl.ANY),
         ],
         out_specs=pl.BlockSpec((rows, CH), lambda g: (g, 0)),
-        scratch_shapes=[VM((BK, CH // HD * rows), F32)] * 2,
+        scratch_shapes=[VM((BK, CH // HD * rows), F32)] * 2
+        + [VM((TOKENS, 2 * HD), BF16), pltpu.SemaphoreType.DMA((NSEQ // GROUP,))],
         compiler_params=pltpu.CompilerParams(vmem_limit_bytes=VLIM),
         name="attend",
     )(positions, lengths, q, kv)

time: 77.5 us -> 77.4 us (level)
    pallas_call x1, Pallas kernels: 15.6 us -> 16.4 us  [attend(): pl.pallas_call(attend_kernel, out_shape=jax.ShapeDtypeStruct((TOK, CH), B...]
where the time goes in v1:
time: 77.4 us; the launch traced here: 77.7 us
  Pallas kernels  76.2 us (98%)
  local copies, waits for them, and re-layouts  0.8 us (1%)
    pallas_call x1, Pallas kernels, mix(): pl.pallas_call(mixer_kernel, out_shape=(jax.ShapeDtypeStruct((TOK, CH), B...  59.8 us
    pallas_call x1, Pallas kernels, attend(): pl.pallas_call(attend_kernel, out_shape=jax.ShapeDtypeStruct((TOK, CH), B...  16.4 us

profile of v1, /device:TPU:1, one launch (start us, length us, event | category | flops | bytes accessed | tf_op | source)
XLA Modules:
  0.0 77.7 jit_solution(2261881621136610736)
XLA Ops:
  0.6 59.8 %mixer.1 = (bf16[256,1024]{1,0:T(8,128)(2,1)}, bf16[8192,256]{1,0:T(8,128)(2,1)}, s32[64,128]{1,0:T(8,128)}, bf16[256,1024]{1,0:T(8,128)(2,1)}) custom-call(s32[64,128]{1,0:T(8,128)} %bitcast.6, s32[4]{0:T(128)} %len_ref.3, bf16[256,1024]{1,0:T(8,128)(2,1)} %q_ref.1, bf16[256,128]{1,0:T(8,128)(2,1)} %k_ref.1, bf16[256,128]{1,0:T(8,128)(2,1)} %v_ref.1, ...), custom_call_target="tpu_custom_call" | custom-call | tf_op jit(solution)/shard_map/mixer/pallas_call | solution.py:541
  60.5 0.0 copy-start
  60.5 16.4 %attend.1 = bf16[256,1024]{1,0:T(8,128)(2,1)} custom-call(s32[64,128]{1,0:T(8,128)} %get-tuple-element.7.pos_ref, s32[4]{0:T(128)} %len_ref.3, bf16[256,1024]{1,0:T(8,128)(2,1)} %get-tuple-element.8.q_ref, bf16[8192,256]{1,0:T(8,128)(2,1)} %get-tuple-element.9.kv_hbm), custom_call_target="tpu_custom_call" | custom-call | tf_op jit(solution)/shard_map/attend/pallas_call | solution.py:720
  76.9 0.0 copy-done
  76.9 0.8 %copy.17 = bf16[256,1024]{1,0:T(8,128)(2,1)} copy(bf16[256,1024]{1,0:T(8,128)(2,1)S(1)} %copy-done) | data formatting | bytes 1048576
Async XLA Ops:
  60.5 16.4 %copy-start = (bf16[256,1024]{1,0:T(8,128)(2,1)S(1)}, bf16[256,1024]{1,0:T(8,128)(2,1)}, u32[]{:S(2)}) copy-start(bf16[256,1024]{1,0:T(8,128)(2,1)} %get-tuple-element.12) | copy-start | bytes 1572868

commit v2 on v1

--- a/solution.py
+++ b/solution.py
@@ -27,7 +27,6 @@
 PROJ = RANK + 2 * NS
 HD = 128
 TAPS = 4
-HALVES = 2
 BIG_STEP = 1.0e7
 MASKED = -1.0e30
 GROUP = 8
@@ -95,10 +94,8 @@
     ext,
     inner,
     part,
-    rs_plus,
-    rs_minus,
-    go_plus,
-    go_minus,
+    taken,
+    onward,
     proj,
     steps,
     drives,
@@ -133,14 +130,20 @@
     me = (x * NY + y) * NC + c
     anchor = me * TOK
     barrier = pltpu.get_barrier_semaphore()
-    for k in range(1, NSEQ):
+    near_x = [lax.rem(x + d, NX) for d in range(NX)]
+    near_y = [lax.rem(y + d, NY) for d in range(NY)]
+    near_z = [lax.rem(z + d, NZ) for d in range(NZ)]
+    near_c = [c, 1 - c]
+    far_first = (2, 1, 3)
+    peers = [
+        (dx, dy, dc) for dx in (*far_first, 0) for dy in (*far_first, 0) for dc in range(NC)
+    ][:-2] + [(0, 0, 1)]
+    for dx, dy, dc in peers:
         pl.semaphore_signal(
-            barrier, inc=1, device_id=seq_device(lax.rem(me + k, NSEQ), z), device_id_type=MESH
+            barrier, inc=1, device_id=(near_x[dx], near_y[dy], near_c[dc], z), device_id_type=MESH
         )
     for k in range(1, NZ):
-        pl.semaphore_signal(
-            barrier, inc=1, device_id=(x, y, c, lax.rem(z + k, NZ)), device_id_type=MESH
-        )
+        pl.semaphore_signal(barrier, inc=1, device_id=(x, y, c, near_z[k]), device_id_type=MESH)
     load_k = pltpu.make_async_copy(k_ref, kvs.at[:, pl.ds(0, HD)], loc_sem.at[0])
     load_k.start()
     load_x = pltpu.make_async_copy(xw_hbm, xw_ref, loc_sem.at[2])
@@ -212,7 +215,7 @@
     load_k.wait()
     mine = kv_out.at[rows_of(0, 0, c)]
     sends = []
-    for a in range(1, NX):
+    for a in far_first:
         px, py = offset(a, 0, c)
         copy = remote(kvs, mine, kv_send.at[a], kv_recv.at[a], (px, py, c, z))
         copy.start()
@@ -223,9 +226,11 @@
     keep_kv = pltpu.make_async_copy(kvs, mine, loc_sem.at[0])
     keep_kv.start()
     q_rows = pl.ds(pl.multiple_of(me * RUN, RUN), RUN)
-    for k in range(1, NSEQ):
-        j = lax.rem(me + k, NSEQ)
-        copy = remote(qs.at[j], q_out.at[q_rows], q_send.at[k], q_recv.at[k], seq_device(j, z))
+    for dx, dy, dc in peers:
+        k = (dx * NY + dy) * NC + dc
+        j = (near_x[dx] * NY + near_y[dy]) * NC + near_c[dc]
+        device = (near_x[dx], near_y[dy], near_c[dc], z)
+        copy = remote(qs.at[j], q_out.at[q_rows], q_send.at[k], q_recv.at[k], device)
         copy.start()
         sends.append(copy)
     keep_q = pltpu.make_async_copy(qs.at[me], q_out.at[q_rows], loc_sem.at[1])
@@ -241,103 +246,80 @@
         inner[...], xw_ref[...], (((1,), (1,)), ((), ())), preferred_element_type=F32
     ).astype(BF16)
     slice_rows = TOK // NZ
-    part_rows = slice_rows // HALVES
-    part[...] = partial.reshape(NZ, HALVES, part_rows, PROJ)
-    up = (x, y, c, lax.rem(z + 1, NZ))
-    down = (x, y, c, lax.rem(z + NZ - 1, NZ))
-
-    def ring_plus(s, h):
-        src = part.at[lax.rem(z + 4, NZ), h] if s == 1 else go_plus.at[s, h]
-        index = h * NZ + s
-        return remote(src, rs_plus.at[s, h], rs_send.at[index], rs_recv.at[index], up)
-
-    def ring_minus(s, h):
-        src = part.at[lax.rem(z + 5, NZ), h] if s == 1 else go_minus.at[s, h]
-        index = h * NZ + 4 + s
-        return remote(src, rs_minus.at[s, h], rs_send.at[index], rs_recv.at[index], down)
+    part[...] = partial.reshape(NZ, slice_rows, PROJ)
 
     def begin(copy):
         copy.start()
         sends.append(copy)
         return copy
 
-    plus, minus = [], []
-    for h in range(HALVES):
-        plus.append(begin(ring_plus(1, h)))
-        minus.append(begin(ring_minus(1, h)))
+    def to_sum(src, slot, d):
+        return remote(
+            src, taken.at[slot], rs_send.at[slot], rs_recv.at[slot], (x, y, c, near_z[d % NZ])
+        )
+
+    far_up = begin(to_sum(part.at[near_z[4]], 1, -2))
+    mid_up = begin(to_sum(part.at[near_z[5]], 0, -1))
+    mid_down = begin(to_sum(part.at[near_z[3]], 2, 1))
+    last = [begin(to_sum(part.at[near_z[7]], 3, -1)), begin(to_sum(part.at[near_z[1]], 4, 1))]
 
     def wait_kv(slot_rows, index):
         remote(kvs, kv_out.at[slot_rows], kv_send.at[0], kv_recv.at[index], partner).wait_recv()
 
-    for s in range(1, 4):
-        for h in range(HALVES):
-            plus[h].wait_recv()
-            ours = part[lax.rem(z + 4 - s, NZ), h].astype(F32)
-            go_plus[s + 1, h] = (rs_plus[s, h].astype(F32) + ours).astype(BF16)
-            plus[h] = begin(ring_plus(s + 1, h))
-            minus[h].wait_recv()
-            if s < 3:
-                ours = part[lax.rem(z + 5 + s, NZ), h].astype(F32)
-                go_minus[s + 1, h] = (rs_minus[s, h].astype(F32) + ours).astype(BF16)
-                minus[h] = begin(ring_minus(s + 1, h))
-        if s == 2:
-            for a in range(NX):
-                if a > 0:
-                    wait_kv(rows_of(-a, 0, c), a)
-                block = kv_out.at[rows_of(-a, 0, c)] if a > 0 else kvs
-                target = kv_out.at[rows_of(-a, 0, c)]
-                for b in range(1, NY):
-                    px, py = offset(0, b, c)
-                    index = b * NX + a
-                    copy = remote(
-                        block, target, kv_send.at[index], kv_recv.at[index], (px, py, c, z)
-                    )
-                    copy.start()
-                    sends.append(copy)
-                if a > 0:
-                    copy = remote(
-                        block, target, kv_send.at[16 + a], kv_recv.at[16 + a], partner
-                    )
-                    copy.start()
-                    sends.append(copy)
-
-    def proj_rows(chunk, h):
-        first = lax.rem(chunk, NZ) * slice_rows + h * part_rows
-        return pl.ds(pl.multiple_of(first, part_rows), part_rows)
-
-    def pass_plus(s, h):
-        rows = proj.at[proj_rows(z + NZ + 1 - s, h)]
-        index = h * NZ + s
-        return remote(rows, rows, ag_send.at[index], ag_recv.at[index], up)
-
-    def pass_minus(s, h):
-        rows = proj.at[proj_rows(z + s - 1, h)]
-        index = h * NZ + 4 + s
-        return remote(rows, rows, ag_send.at[index], ag_recv.at[index], down)
-
-    def got_plus(s, h):
-        rows = proj.at[proj_rows(z + NZ - s, h)]
-        index = h * NZ + s
-        remote(rows, rows, ag_send.at[index], ag_recv.at[index], up).wait_recv()
-
-    def got_minus(s, h):
-        rows = proj.at[proj_rows(z + s, h)]
-        index = h * NZ + 4 + s
-        remote(rows, rows, ag_send.at[index], ag_recv.at[index], down).wait_recv()
-
-    for h in range(HALVES):
-        plus[h].wait_recv()
-        total = part[z, h].astype(F32) + rs_plus[4, h].astype(F32) + rs_minus[3, h].astype(F32)
-        proj[proj_rows(z, h), :] = total.astype(BF16)
-        begin(pass_plus(1, h))
-        begin(pass_minus(1, h))
-    for s in range(2, 5):
-        for h in range(HALVES):
-            got_plus(s - 1, h)
-            begin(pass_plus(s, h))
-            if s < 4:
-                got_minus(s - 1, h)
-                begin(pass_minus(s, h))
+    mid_down.wait_recv()
+    onward[1] = (part[near_z[2]].astype(F32) + taken[2].astype(F32)).astype(BF16)
+    last.append(begin(to_sum(onward.at[1], 6, 2)))
+    mid_up.wait_recv()
+    far_up.wait_recv()
+    merged = part[near_z[6]].astype(F32) + taken[0].astype(F32) + taken[1].astype(F32)
+    onward[0] = merged.astype(BF16)
+    last.append(begin(to_sum(onward.at[0], 5, -2)))
+    for a in range(NX):
+        if a > 0:
+            wait_kv(rows_of(-a, 0, c), a)
+        block = kv_out.at[rows_of(-a, 0, c)] if a > 0 else kvs
+        target = kv_out.at[rows_of(-a, 0, c)]
+        for b in far_first:
+            px, py = offset(0, b, c)
+            index = b * NX + a
+            copy = remote(
+                block, target, kv_send.at[index], kv_recv.at[index], (px, py, c, z)
+            )
+            copy.start()
+            sends.append(copy)
+        if a > 0:
+            copy = remote(
+                block, target, kv_send.at[16 + a], kv_recv.at[16 + a], partner
+            )
+            copy.start()
+            sends.append(copy)
+
+
+    total = part[z].astype(F32)
+    for copy in last:
+        copy.wait_recv()
+    for slot in range(3, 7):
+        total = total + taken[slot].astype(F32)
+
+    def proj_rows(d):
+        return pl.ds(pl.multiple_of(near_z[d % NZ] * slice_rows, slice_rows), slice_rows)
+
+    def to_gather(chunk, index, d):
+        rows = proj.at[proj_rows(chunk)]
+        return remote(
+            rows, rows, ag_send.at[index], ag_recv.at[index], (x, y, c, near_z[d % NZ])
+        )
+
+    proj[proj_rows(0), :] = total.astype(BF16)
+    begin(to_gather(0, 0, 2))
+    begin(to_gather(0, 1, -2))
+    begin(to_gather(0, 2, 1))
+    begin(to_gather(0, 3, -1))
+    to_gather(-2, 0, 2).wait_recv()
+    begin(to_gather(-2, 4, 2))
+    begin(to_gather(-2, 5, 1))
+    to_gather(2, 1, -2).wait_recv()
+    begin(to_gather(2, 6, -1))
     spots = (TOKENS // LANE, LANE)
     spot = lax.broadcasted_iota(jnp.int32, spots, 1)
     ours = (lax.shift_right_logical(dest_ref[...], TOK_BITS) == me) & (spot % RUN == 0)
@@ -347,9 +329,8 @@
     for j in range(SUB):
         cols = pl.ds(j * LANE, LANE)
         rates[pl.ds(j, NS, stride=SUB), :] = rate_ref[:, cols] * (-LOG2E)
-    for h in range(HALVES):
-        got_minus(3, h)
-        got_plus(4, h)
+    for chunk, index in ((-1, 2), (1, 3), (-4, 4), (-3, 5), (3, 6)):
+        to_gather(chunk, index, 1).wait_recv()
 
     load_d.wait()
     begins = depth == 0
@@ -455,9 +436,9 @@
     chip_state = follow(early, late, late_total)
     pack(st_y.at[0], chip_state, own_total + other_total)
     level = []
-    for k in range(1, NY):
+    for k in far_first:
         copy = remote(
-            st_y.at[0], st_y.at[k], st_send.at[k], st_recv.at[k], (x, lax.rem(y + k, NY), c, z)
+            st_y.at[0], st_y.at[k], st_send.at[k], st_recv.at[k], (x, near_y[k], c, z)
         )
         copy.start()
         level.append(copy)
@@ -473,9 +454,9 @@
         column_total = column_total + total
     pack(st_x.at[0], column, column_total)
     level = []
-    for k in range(1, NX):
+    for k in far_first:
         copy = remote(
-            st_x.at[0], st_x.at[k], st_send.at[4 + k], st_recv.at[4 + k], (lax.rem(x + k, NX), y, c, z)
+            st_x.at[0], st_x.at[k], st_send.at[4 + k], st_recv.at[4 + k], (near_x[k], y, c, z)
         )
         copy.start()
         level.append(copy)
@@ -522,8 +503,10 @@
         cols = pl.ds(j * LANE, LANE)
         out[:, cols] = (ys[pl.ds(j, TOK, stride=SUB), :] * gates[:, cols]).astype(BF16)
 
-    for k in range(1, NSEQ):
-        rows = pl.ds(pl.multiple_of(lax.rem(me + NSEQ - k, NSEQ) * RUN, RUN), RUN)
+    for dx, dy, dc in peers:
+        k = (dx * NY + dy) * NC + dc
+        source = (near_x[-dx % NX] * NY + near_y[-dy % NY]) * NC + near_c[dc]
+        rows = pl.ds(pl.multiple_of(source * RUN, RUN), RUN)
         remote(qs.at[0], q_out.at[rows], q_send.at[k], q_recv.at[k], partner).wait_recv()
     for b in range(NY):
         for a in range(NX):
@@ -537,7 +520,7 @@
 def mix(dest, lengths, q, k, v, x, z, cw, cb, xw, dtw, dtb, rate, skip):
     dma = pltpu.SemaphoreType.DMA
     states = ((NS + 2) * SUB, LANE)
-    chunk = (HALVES, TOK // NZ // HALVES, PROJ)
+    chunk = (TOK // NZ, PROJ)
     return pl.pallas_call(
         mixer_kernel,
         out_shape=(
@@ -568,10 +551,8 @@
             VM((TOK + 8, CH), F32),
             VM((TOK, CH), BF16),
             VM((NZ, *chunk), BF16),
-            VM((5, *chunk), BF16),
-            VM((4, *chunk), BF16),
-            VM((5, *chunk), BF16),
-            VM((4, *chunk), BF16),
+            VM((NZ, *chunk), BF16),
+            VM((2, *chunk), BF16),
             VM((TOK, PROJ), BF16),
             VM((TOK * SUB, LANE), F32),
             VM((TOK * SUB, LANE), F32),
@@ -595,10 +576,10 @@
             dma((32,)),
             dma((NSEQ,)),
             dma((NSEQ,)),
-            dma((HALVES * NZ,)),
-            dma((HALVES * NZ,)),
-            dma((HALVES * NZ,)),
-            dma((HALVES * NZ,)),
+            dma((NZ,)),
+            dma((NZ,)),
+            dma((NZ,)),
+            dma((NZ,)),
             dma((NZ,)),
             dma((NZ,)),
         ],

time: 77.4 us -> 70.7 us (0.913); the launches traced: 77.7 us -> 71.9 us
  Pallas kernels: 76.2 us -> 70.4 us
    pallas_call x1, Pallas kernels: 59.8 us -> 52.3 us  [mix(): pl.pallas_call(mixer_kernel, out_shape=(jax.ShapeDtypeStruct((TOK, CH), B...]
    pallas_call x1, Pallas kernels: 16.4 us -> 18.1 us  [attend(): pl.pallas_call(attend_kernel, out_shape=jax.ShapeDtypeStruct((TOK, CH), B...]
where the time goes in v2:
time: 70.7 us; the launch traced here: 71.9 us
  Pallas kernels  70.4 us (100%)
  local copies, waits for them, and re-layouts  0.8 us (1%)
    pallas_call x1, Pallas kernels, mix(): pl.pallas_call(mixer_kernel, out_shape=(jax.ShapeDtypeStruct((TOK, CH), B...  52.3 us
    pallas_call x1, Pallas kernels, attend(): pl.pallas_call(attend_kernel, out_shape=jax.ShapeDtypeStruct((TOK, CH), B...  18.1 us

profile of v2, /device:TPU:1, one launch (start us, length us, event | category | flops | bytes accessed | tf_op | source)
XLA Modules:
  0.0 71.9 jit_solution(14419858094830932113)
XLA Ops:
  0.6 52.3 %mixer.1 = (bf16[256,1024]{1,0:T(8,128)(2,1)}, bf16[8192,256]{1,0:T(8,128)(2,1)}, s32[64,128]{1,0:T(8,128)}, bf16[256,1024]{1,0:T(8,128)(2,1)}) custom-call(s32[64,128]{1,0:T(8,128)} %bitcast.6, s32[4]{0:T(128)} %len_ref.3, bf16[256,1024]{1,0:T(8,128)(2,1)} %q_ref.1, bf16[256,128]{1,0:T(8,128)(2,1)} %k_ref.1, bf16[256,128]{1,0:T(8,128)(2,1)} %v_ref.1, ...), custom_call_target="tpu_custom_call" | custom-call | tf_op jit(solution)/shard_map/mixer/pallas_call | solution.py:524
  52.9 0.0 copy-start
  53.0 18.1 %attend.1 = bf16[256,1024]{1,0:T(8,128)(2,1)} custom-call(s32[64,128]{1,0:T(8,128)} %get-tuple-element.7.pos_ref, s32[4]{0:T(128)} %len_ref.3, bf16[256,1024]{1,0:T(8,128)(2,1)} %get-tuple-element.8.q_ref, bf16[8192,256]{1,0:T(8,128)(2,1)} %get-tuple-element.9.kv_hbm), custom_call_target="tpu_custom_call" | custom-call | tf_op jit(solution)/shard_map/attend/pallas_call | solution.py:701
  71.1 0.0 copy-done
  71.1 0.8 %copy.17 = bf16[256,1024]{1,0:T(8,128)(2,1)} copy(bf16[256,1024]{1,0:T(8,128)(2,1)S(1)} %copy-done) | data formatting | bytes 1048576
Async XLA Ops:
  52.9 18.1 %copy-start = (bf16[256,1024]{1,0:T(8,128)(2,1)S(1)}, bf16[256,1024]{1,0:T(8,128)(2,1)}, u32[]{:S(2)}) copy-start(bf16[256,1024]{1,0:T(8,128)(2,1)} %get-tuple-element.12) | copy-start | bytes 1572868
